TPU v7x, 256 devices: a whole 4x4x8 slice. The times are simulated.
256 devices in a mesh: seq: 32 (over z, y_hi, core), chan: 8 (over y_lo, x).
Axes of the slice: x: 4, y: 4 (y_hi: 2, y_lo: 2; y = y_hi * 2 + y_lo), z: 8, core: 2. Of those that a mesh axis runs over, the one named last changes fastest.
Arguments:
- tokens: bfloat16 [384, 512, 1024], P('chan', 'seq'), may hold values from -6 to 6
- gating: bfloat16 [384, 512, 1024], P(None, ('seq', 'chan')), may hold values from -6 to 6
- kernel: bfloat16 [384, 1024, 512], P('chan', 'seq'), may hold values from -6 to 6
- first_factor: bfloat16 [1024, 1024], replicated, may hold values from -0.1875 to 0.1875
- first_twiddle: float32 [512, 1024], P('seq'), may hold values from 0.5 to 1.5
- second_factor: bfloat16 [512, 512], replicated, may hold values from -0.25 to 0.25
- inverse_second: bfloat16 [512, 512], replicated, may hold values from -0.25 to 0.25
- inverse_twiddle: float32 [1024, 512], P('seq'), may hold values from 0.5 to 1.5
- inverse_first: bfloat16 [1024, 1024], replicated, may hold values from -0.1875 to 0.1875
- projection: bfloat16 [384, 384], replicated, may hold values from -0.3125 to 0.3125
Outputs:
- result: bfloat16 [384, 512, 1024], P(None, ('seq', 'chan'))
All inputs are finite; a program needn't handle non-finite values.
Results may differ from a plain program's by a relative error of at most 0.012.
Values may be sent and summed in bfloat16 or wider, within the bound.
A program may use at most 64 MiB of HBM per device.

v0:
```python
import functools

import jax
import jax.numpy as jnp
from jax import lax
from jax.experimental import pallas as pl
from jax.experimental.pallas import tpu as pltpu
from jax.sharding import PartitionSpec as P

MESH = pl.DeviceIdType.MESH
F32 = jnp.float32
BF16 = jnp.bfloat16
SEQ, CHAN = 32, 8
CL, AL, B, A, KL, D = 48, 16, 1024, 512, 32, 384
CH = 16
NH = CL // CH
WH = CH * KL
CQ = 8
NQ = CL // CQ
W = CQ * KL
FAR = [d for k in range(17) for d in sorted({16 - k, 16 + k}) if 0 < d < SEQ]


def nt(a, b):
    return lax.dot_general(a, b, (((1,), (1,)), ((), ())), preferred_element_type=F32)


def swap_groups(v, hi, odd):
    v0, v1, v2, v3 = v
    a0 = jnp.where(hi, pltpu.roll(v2, 64, 1), v0)
    a2 = jnp.where(hi, v2, pltpu.roll(v0, 64, 1))
    a1 = jnp.where(hi, pltpu.roll(v3, 64, 1), v1)
    a3 = jnp.where(hi, v3, pltpu.roll(v1, 64, 1))
    o0 = jnp.where(odd, pltpu.roll(a1, 32, 1), a0)
    o1 = jnp.where(odd, a1, pltpu.roll(a0, 96, 1))
    o2 = jnp.where(odd, pltpu.roll(a3, 32, 1), a2)
    o3 = jnp.where(odd, a3, pltpu.roll(a2, 96, 1))
    return o0, o1, o2, o3


def at(i, n):
    return pl.ds(pl.multiple_of(i * n, n), n)


def mixer(
    tok_h, gat_h, ker_h, f1_h, tw1_h, s2_h, v2_h, tw2_h, u1_h, pr_h,
    gd, pt,
    tok, gat, ker, f1, tw1, s2, v2, tw2, u1, pr,
    snd1, xin, cnd, cin, snd2, zin, kt_, tw2t, v2p, tw2p, gp, lb, sf, sp,
    fsem, tsem, lsem, ssem, xsem, csem, zsem,
):
    me = lax.axis_index("seq")
    mc = lax.axis_index("chan")
    n0 = lax.rem(lax.div(me, 8) + 2, 4)

    def f1_load(i):
        rows = at(lax.rem(n0 + i, 4), 256)
        return pltpu.make_async_copy(f1_h.at[rows], f1.at[rows], fsem.at[i])

    def tok_load(h):
        rows = pl.ds(h * CH, CH)
        return pltpu.make_async_copy(tok_h.at[rows], tok.at[rows], tsem.at[h])

    loads = [
        pltpu.make_async_copy(src, dst, lsem.at[i])
        for i, (src, dst) in enumerate(
            [(tw1_h, tw1), (s2_h, s2), (ker_h, ker), (v2_h, v2), (tw2_h, tw2), (u1_h, u1), (pr_h, pr)]
            + [(gat_h.at[pl.ds(p * CL, CL)], gat.at[:, p]) for p in range(CHAN)]
        )
    ]
    tok_load(0).start()
    f1_load(0).start()
    loads[0].start()

    barrier = pltpu.get_barrier_semaphore()
    for d in FAR:
        pl.semaphore_signal(barrier, inc=1, device_id={"seq": lax.rem(me + d, SEQ)}, device_id_type=MESH)
    for d in range(1, CHAN):
        pl.semaphore_signal(barrier, inc=1, device_id={"chan": lax.rem(mc + d, CHAN)}, device_id_type=MESH)

    for i in range(1, 4):
        f1_load(i).start()
    for h in range(1, NH):
        tok_load(h).start()
    for c in loads[1:]:
        c.start()

    lane = lax.broadcasted_iota(jnp.int32, (16, 128), 1)
    hi = lane >= 64
    odd = lax.rem(lax.div(lane, 32), 2) == 1

    def send(src, dst, sem, p, lanes):
        pltpu.make_async_remote_copy(
            src.at[p, :, lanes], dst.at[me, :, lanes], ssem.at[0], sem,
            device_id={"seq": p}, device_id_type=MESH,
        ).start()

    def arrived(dst, sem, lanes):
        block = dst.at[pl.ds(0, SEQ - 1), :, lanes]
        pltpu.make_async_copy(block, block, sem).wait()

    loads[0].wait()
    for h in range(NH):
        tok_load(h).wait()
        lanes = pl.ds(h * WH, WH)

        def first(i, c, h=h, lanes=lanes):
            n = lax.rem(n0 + i, 4)
            if h == 0:
                f1_load(i).wait()
            rows = tok[pl.ds(h * CH, CH)].reshape(CH * AL, B)
            f = nt(rows, f1[at(n, 256), :])
            for t in range(2):
                tw = tw1[:, at(2 * n + t, 128)]
                for g in range(CH // 4):
                    tiles = [f[(4 * g + j) * 16:(4 * g + j + 1) * 16, t * 128:(t + 1) * 128] * tw for j in range(4)]
                    outs = swap_groups(tiles, hi, odd)
                    for j in range(4):
                        snd1[n * 8 + t * 4 + j, :, h * WH + g * 128:h * WH + (g + 1) * 128] = outs[j].astype(BF16)
            if h == 0:
                @pl.when(i == 0)
                def _():
                    pl.semaphore_wait(barrier, SEQ - 1 + CHAN - 1)
            for j in range(8):
                p = n * 8 + j

                @pl.when(p != me)
                def _(p=p):
                    send(snd1, xin, xsem.at[h], p, lanes)

            return c

        lax.fori_loop(0, 4, first, 0)
        xin[me, :, lanes] = snd1[me, :, lanes]

    for c in loads[1:]:
        c.wait()

    def flip(q, c):
        k = ker[pl.ds(q * CQ, CQ)].reshape(W, A)
        kt_[q] = k.T
        return c

    lax.fori_loop(0, NQ, flip, 0)
    t = tw2[...]
    tw2t[...] = jnp.concatenate([t, t, t, t], axis=0).T
    for k in range(A // 128):
        sf[...] = v2[:, k * 128:(k + 1) * 128].astype(F32)

        def order(i, c, k=k):
            v2p[at(i, SEQ), k * 128:(k + 1) * 128] = sf[pl.ds(i, SEQ, stride=16), :].astype(BF16)
            if k == 0:
                tw2p[at(i, SEQ), :] = tw2t[pl.ds(i, SEQ, stride=16), :]
            return c

        lax.fori_loop(0, 16, order, 0)

    def middle(q):
        lanes = at(q, W)
        x = xin[:, :, lanes].reshape(A, W)
        spectrum = jnp.dot(s2[...], x, preferred_element_type=F32)
        scaled = (spectrum * kt_[q].astype(F32)).astype(BF16)
        inv = jnp.dot(v2p[...], scaled, preferred_element_type=F32)
        tw = tw2p[...]
        inv = (inv * jnp.concatenate([tw] * (W // 128), axis=1)).astype(BF16)
        cnd[q] = inv.reshape(CHAN, 64, W)
        cin[q, mc] = cnd[q, mc]
        for d in (4, 1, 5, 7, 3, 2, 6):
            p = lax.rem(mc + d, CHAN)
            pltpu.make_async_remote_copy(
                cnd.at[q, p], cin.at[q, mc], ssem.at[1], csem.at[q],
                device_id={"chan": p}, device_id_type=MESH,
            ).start()

    def onward(q):
        block = cin.at[q, pl.ds(0, CHAN - 1)]
        pltpu.make_async_copy(block, block, csem.at[q]).wait()
        for t in range(W // 128):
            cols = slice(t * 128, (t + 1) * 128)
            for r in range(2):
                for p in range(CHAN):
                    sf[(r * 8 + p) * 32:(r * 8 + p + 1) * 32, :] = cin[q, p, r * 32:(r + 1) * 32, cols].astype(F32)

            def pick(s, c, t=t):
                snd2[s, :, at(q * (W // 128) + t, 128)] = sf[pl.ds(s, 16, stride=SEQ), :].astype(BF16)
                return c

            lax.fori_loop(0, SEQ, pick, 0, unroll=8)
        lanes = at(q, W)
        zin[me, :, lanes] = snd2[me, :, lanes]
        for d in FAR:
            send(snd2, zin, zsem.at[q], lax.rem(me + d, SEQ), lanes)

    def stage(q, c):
        @pl.when(lax.rem(q, 2) == 0)
        def _():
            h = lax.div(q, 2)
            arrived(xin, xsem.at[h], at(h, WH))

        middle(q)

        @pl.when(q > 0)
        def _():
            onward(q - 1)

        return c

    lax.fori_loop(0, NQ, stage, 0)
    onward(NQ - 1)

    def gate_rows(i, c):
        g = gat[i].astype(F32)
        gp[at(i, 16), :] = jnp.concatenate([g[:, 0, :], g[:, 1, :]], axis=0).astype(BF16)
        return c

    lax.fori_loop(0, CL, gate_rows, 0)
    for k in range(D // 128):
        for p in range(CHAN):
            sp[pl.ds(p, CL, stride=CHAN), :] = pr[p * CL:(p + 1) * CL, k * 128:(k + 1) * 128].astype(F32)
        pt[k * 128:(k + 1) * 128, :] = sp[...].T.astype(BF16)

    def mix(q, c):
        arrived(zin, zsem.at[q], at(q, W))

        def regroup(k, c):
            for g in range(CQ // 4):
                lanes = at(q * (CQ // 4) + g, 128)
                tiles = [zin[4 * k + j, :, lanes].astype(F32) for j in range(4)]
                outs = swap_groups(tiles, hi, odd)
                for j in range(4):
                    lb[(4 * g + j) * 16:(4 * g + j + 1) * 16, at(k, 128)] = outs[j].astype(BF16)
            return c

        lax.fori_loop(0, B // 128, regroup, 0)

        def columns(n, c):
            cols = at(n, 256)
            m = nt(lb[...], u1[cols, :]).astype(BF16).astype(F32)
            m = m * gp[at(q, CQ * 16), cols].astype(F32)
            m = m.reshape(CQ, 2, CHAN, 256)
            for r in range(2):
                gd[r, at(q, CQ * CHAN), cols] = m[:, r].reshape(CQ * CHAN, 256).astype(BF16)
            return c

        lax.fori_loop(0, B // 256, columns, 0)
        return c

    lax.fori_loop(0, NQ, mix, 0)

    for buf in (snd1, snd2):
        block = buf.at[pl.ds(0, SEQ - 1)]
        pltpu.make_async_copy(block, block, ssem.at[0]).wait()
    block = cnd.at[:, pl.ds(0, CHAN - 1)]
    pltpu.make_async_copy(block, block, ssem.at[1]).wait()


def projector(gd, pt, out_h, res, sem):
    copies = []
    for n in range(B // 256):
        cols = slice(n * 256, (n + 1) * 256)
        for r in range(2):
            res[n, :, r, :] = jnp.dot(pt[...], gd[r, :, cols], preferred_element_type=F32).astype(BF16)
        copies.append(pltpu.make_async_copy(res.at[n], out_h.at[:, :, pl.ds(n * 256, 256)], sem.at[n]))
        copies[-1].start()
    for c in copies:
        c.wait()


def body(*args):
    hbm = pl.BlockSpec(memory_space=pltpu.HBM)
    whole = pl.BlockSpec(memory_space=pltpu.VMEM)
    vm = pltpu.VMEM
    dma = pltpu.SemaphoreType.DMA
    gd, pt = pl.pallas_call(
        mixer,
        out_shape=(jax.ShapeDtypeStruct((2, D, B), BF16), jax.ShapeDtypeStruct((D, D), BF16)),
        in_specs=[hbm] * 10,
        out_specs=(whole, whole),
        scratch_shapes=[
            vm((CL, AL, B), BF16), vm((CL, CHAN, 2, B), BF16), vm((CL, KL, A), BF16), vm((B, B), BF16),
            vm((AL, B), F32), vm((A, A), BF16), vm((A, A), BF16), vm((KL, A), F32), vm((B, B), BF16), vm((D, D), BF16),
            vm((SEQ, 16, CL * KL), BF16), vm((SEQ, 16, CL * KL), BF16),
            vm((NQ, CHAN, 64, W), BF16), vm((NQ, CHAN, 64, W), BF16),
            vm((SEQ, 16, CL * KL), BF16), vm((SEQ, 16, CL * KL), BF16),
            vm((NQ, A, W), BF16), vm((A, 128), F32), vm((A, A), BF16), vm((A, 128), F32),
            vm((CL * 16, B), BF16), vm((16 * CQ, B), BF16), vm((A, 128), F32), vm((D, 128), F32),
            dma((4,)), dma((NH,)), dma((15,)), dma((2,)), dma((NH,)), dma((NQ,)), dma((NQ,)),
        ],
        compiler_params=pltpu.CompilerParams(
            collective_id=0, has_side_effects=True, vmem_limit_bytes=VLIM * 1024 * 1024
        ),
    )(*[pltpu.with_memory_space_constraint(x, pltpu.HBM) for x in args])
    return pl.pallas_call(
        projector,
        out_shape=jax.ShapeDtypeStruct((D, 2, B), BF16),
        in_specs=[whole, whole],
        out_specs=hbm,
        scratch_shapes=[vm((B // 256, D, 2, 256), BF16), dma((B // 256,))],
        compiler_params=pltpu.CompilerParams(vmem_limit_bytes=32 * 1024 * 1024),
    )(gd, pt)


VLIM = 48


def solution(mesh):
    return jax.shard_map(
        body,
        mesh=mesh,
        in_specs=(
            P("chan", "seq", None),
            P(None, ("seq", "chan"), None),
            P("chan", "seq", None),
            P(),
            P("seq", None),
            P(),
            P(),
            P("seq", None),
            P(),
            P(),
        ),
        out_specs=P(None, ("seq", "chan"), None),
        check_vma=False,
    )
```

profile of v0, /device:TPU:1, one launch (start us, length us, event | category | flops | bytes accessed | tf_op | source)
XLA Modules:
  0.0 87.1 jit_solution(17412772623570396827)
XLA Ops:
  0.0 84.1 %shard_map.100 = (bf16[2,384,1024]{2,1,0:T(8,128)(2,1)S(1)}, bf16[384,384]{1,0:T(8,128)(2,1)S(1)}) custom-call(bf16[48,16,1024]{2,1,0:T(8,128)(2,1)} %tok_h.1, bf16[384,2,1024]{2,1,0:T(2,128)(2,1)} %gat_h.1, bf16[48,32,512]{2,1,0:T(8,128)(2,1)} %ker_h.1, bf16[1024,1024]{1,0:T(8,128)(2,1)} %f1_h.1, f32[16,1024]{1,0:T(8,128)} %tw1_h.1, bf16[512,512]{1,0:T(8,128)(2,1)} %s2_h.1, ...), custom_call_target="tpu_custom_call" | custom-call | tf_op jit(solution)/shard_map/pallas_call | solution.py:274
  84.1 3.1 %shard_map.101 = bf16[384,2,1024]{2,1,0:T(2,128)(2,1)} custom-call(bf16[2,384,1024]{2,1,0:T(8,128)(2,1)S(1)} %get-tuple-element.7.gd, bf16[384,384]{1,0:T(8,128)(2,1)S(1)} %get-tuple-element.8.pt), custom_call_target="tpu_custom_call" | custom-call | tf_op jit(solution)/shard_map/pallas_call | solution.py:293
where the time goes:
time: 87.2 us; the launch traced here: 87.1 us
  Pallas kernels  87.1 us (100%)
    pallas_call x1, Pallas kernels, body(): pl.pallas_call(mixer, out_shape=(jax.ShapeDtypeStruct((2, D, B), BF16), j...  84.1 us
    pallas_call x1, Pallas kernels, body(): pl.pallas_call(projector, out_shape=jax.ShapeDtypeStruct((D, 2, B), BF16)...  3.06 us

commit v1 on v0

--- a/solution.py
+++ b/solution.py
@@ -44,9 +44,9 @@
 
 def mixer(
     tok_h, gat_h, ker_h, f1_h, tw1_h, s2_h, v2_h, tw2_h, u1_h, pr_h,
-    gd, pt,
+    acc, pb5, g5,
     tok, gat, ker, f1, tw1, s2, v2, tw2, u1, pr,
-    snd1, xin, cnd, cin, snd2, zin, kt_, tw2t, v2p, tw2p, gp, lb, sf, sp,
+    snd1, xin, cnd, cin, snd2, zin, kt_, tw2t, v2p, tw2p, gp, lb, sf, sp, st, sb, pb, g4,
     fsem, tsem, lsem, ssem, xsem, csem, zsem,
 ):
     me = lax.axis_index("seq")
@@ -172,6 +172,21 @@
                 device_id={"chan": p}, device_id_type=MESH,
             ).start()
 
+    r4 = lax.rem(me, 4)
+
+    def group(q, zs):
+        for zz in zs:
+            for dr in range(4):
+                p = zz * 4 + lax.rem(r4 + dr, 4)
+
+                @pl.when(p != me)
+                def _(p=p):
+                    send(snd2, zin, zsem.at[q], p, at(q, W))
+
+    def far(q):
+        for d in FAR:
+            send(snd2, zin, zsem.at[q], lax.rem(me + d, SEQ), at(q, W))
+
     def onward(q):
         block = cin.at[q, pl.ds(0, CHAN - 1)]
         pltpu.make_async_copy(block, block, csem.at[q]).wait()
@@ -188,8 +203,28 @@
             lax.fori_loop(0, SEQ, pick, 0, unroll=8)
         lanes = at(q, W)
         zin[me, :, lanes] = snd2[me, :, lanes]
-        for d in FAR:
-            send(snd2, zin, zsem.at[q], lax.rem(me + d, SEQ), lanes)
+        group(q, range(8))
+
+    def gate_rows(i, c):
+        g = gat[i].astype(F32)
+        gp[at(i, 16), :] = jnp.concatenate([g[:, 0, :], g[:, 1, :]], axis=0).astype(BF16)
+        return c
+
+    row_of = lax.rem(lax.div(lax.broadcasted_iota(jnp.int32, (128, 128), 1), CHAN), 2)
+
+    def project_rows(k, c):
+        for p in range(CHAN):
+            for r in range(2):
+                sp[pl.ds(r * CHAN + p, CL, stride=2 * CHAN), :] = pr[p * CL:(p + 1) * CL, at(k, 128)].astype(F32)
+        st[...] = sp[...].T
+        for q in range(NQ):
+            for r in range(2):
+                sb[pl.ds(r, 128, stride=2), :] = jnp.where(row_of == r, st[:, q * 128:(q + 1) * 128], 0.0)
+            if q < NQ - 1:
+                pb[q, at(k, 256), :] = sb[...].astype(BF16)
+            else:
+                pb5[at(k, 256), :] = sb[...].astype(BF16)
+        return c
 
     def stage(q, c):
         @pl.when(lax.rem(q, 2) == 0)
@@ -205,21 +240,15 @@
 
         return c
 
-    lax.fori_loop(0, NQ, stage, 0)
+    lax.fori_loop(0, 2, stage, 0)
+    lax.fori_loop(0, CL, gate_rows, 0)
+    lax.fori_loop(2, 4, stage, 0)
+    lax.fori_loop(0, D // 128, project_rows, 0)
+    acc[...] = jnp.zeros_like(acc)
+    lax.fori_loop(4, NQ, stage, 0)
     onward(NQ - 1)
 
-    def gate_rows(i, c):
-        g = gat[i].astype(F32)
-        gp[at(i, 16), :] = jnp.concatenate([g[:, 0, :], g[:, 1, :]], axis=0).astype(BF16)
-        return c
-
-    lax.fori_loop(0, CL, gate_rows, 0)
-    for k in range(D // 128):
-        for p in range(CHAN):
-            sp[pl.ds(p, CL, stride=CHAN), :] = pr[p * CL:(p + 1) * CL, k * 128:(k + 1) * 128].astype(F32)
-        pt[k * 128:(k + 1) * 128, :] = sp[...].T.astype(BF16)
-
-    def mix(q, c):
+    def mix(q, g):
         arrived(zin, zsem.at[q], at(q, W))
 
         def regroup(k, c):
@@ -231,21 +260,30 @@
                     lb[(4 * g + j) * 16:(4 * g + j + 1) * 16, at(k, 128)] = outs[j].astype(BF16)
             return c
 
-        lax.fori_loop(0, B // 128, regroup, 0)
+        lax.fori_loop(0, B // 128, regroup, 0, unroll=UNROLL)
 
         def columns(n, c):
             cols = at(n, 256)
             m = nt(lb[...], u1[cols, :]).astype(BF16).astype(F32)
             m = m * gp[at(q, CQ * 16), cols].astype(F32)
-            m = m.reshape(CQ, 2, CHAN, 256)
-            for r in range(2):
-                gd[r, at(q, CQ * CHAN), cols] = m[:, r].reshape(CQ * CHAN, 256).astype(BF16)
-            return c
-
-        lax.fori_loop(0, B // 256, columns, 0)
-        return c
-
-    lax.fori_loop(0, NQ, mix, 0)
+            g[:, cols] = m.astype(BF16)
+            return c
+
+        lax.fori_loop(0, B // 256, columns, 0, unroll=UNROLL)
+
+    def mix_add(q, c):
+        mix(q, g4)
+
+        def add(n, c):
+            cols = at(n, 256)
+            acc[:, cols] += jnp.dot(pb[q], g4[:, cols], preferred_element_type=F32)
+            return c
+
+        lax.fori_loop(0, B // 256, add, 0)
+        return c
+
+    lax.fori_loop(0, NQ - 1, mix_add, 0)
+    mix(NQ - 1, g5)
 
     for buf in (snd1, snd2):
         block = buf.at[pl.ds(0, SEQ - 1)]
@@ -254,12 +292,12 @@
     pltpu.make_async_copy(block, block, ssem.at[1]).wait()
 
 
-def projector(gd, pt, out_h, res, sem):
+def projector(acc, pb5, g5, out_h, res, sem):
     copies = []
     for n in range(B // 256):
         cols = slice(n * 256, (n + 1) * 256)
-        for r in range(2):
-            res[n, :, r, :] = jnp.dot(pt[...], gd[r, :, cols], preferred_element_type=F32).astype(BF16)
+        v = acc[:, cols] + jnp.dot(pb5[...], g5[:, cols], preferred_element_type=F32)
+        res[n] = v.astype(BF16).reshape(D, 2, 256)
         copies.append(pltpu.make_async_copy(res.at[n], out_h.at[:, :, pl.ds(n * 256, 256)], sem.at[n]))
         copies[-1].start()
     for c in copies:
@@ -271,11 +309,15 @@
     whole = pl.BlockSpec(memory_space=pltpu.VMEM)
     vm = pltpu.VMEM
     dma = pltpu.SemaphoreType.DMA
-    gd, pt = pl.pallas_call(
+    parts = pl.pallas_call(
         mixer,
-        out_shape=(jax.ShapeDtypeStruct((2, D, B), BF16), jax.ShapeDtypeStruct((D, D), BF16)),
+        out_shape=(
+            jax.ShapeDtypeStruct((2 * D, B), F32),
+            jax.ShapeDtypeStruct((2 * D, 128), BF16),
+            jax.ShapeDtypeStruct((128, B), BF16),
+        ),
         in_specs=[hbm] * 10,
-        out_specs=(whole, whole),
+        out_specs=(whole, whole, whole),
         scratch_shapes=[
             vm((CL, AL, B), BF16), vm((CL, CHAN, 2, B), BF16), vm((CL, KL, A), BF16), vm((B, B), BF16),
             vm((AL, B), F32), vm((A, A), BF16), vm((A, A), BF16), vm((KL, A), F32), vm((B, B), BF16), vm((D, D), BF16),
@@ -283,7 +325,8 @@
             vm((NQ, CHAN, 64, W), BF16), vm((NQ, CHAN, 64, W), BF16),
             vm((SEQ, 16, CL * KL), BF16), vm((SEQ, 16, CL * KL), BF16),
             vm((NQ, A, W), BF16), vm((A, 128), F32), vm((A, A), BF16), vm((A, 128), F32),
-            vm((CL * 16, B), BF16), vm((16 * CQ, B), BF16), vm((A, 128), F32), vm((D, 128), F32),
+            vm((CL * 16, B), BF16), vm((16 * CQ, B), BF16), vm((A, 128), F32), vm((2 * D, 128), F32),
+            vm((128, 2 * D), F32), vm((256, 128), F32), vm((NQ - 1, 2 * D, 128), BF16), vm((128, B), BF16),
             dma((4,)), dma((NH,)), dma((15,)), dma((2,)), dma((NH,)), dma((NQ,)), dma((NQ,)),
         ],
         compiler_params=pltpu.CompilerParams(
@@ -293,14 +336,15 @@
     return pl.pallas_call(
         projector,
         out_shape=jax.ShapeDtypeStruct((D, 2, B), BF16),
-        in_specs=[whole, whole],
+        in_specs=[whole, whole, whole],
         out_specs=hbm,
         scratch_shapes=[vm((B // 256, D, 2, 256), BF16), dma((B // 256,))],
         compiler_params=pltpu.CompilerParams(vmem_limit_bytes=32 * 1024 * 1024),
-    )(gd, pt)
+    )(*parts)
 
 
 VLIM = 48
+UNROLL = True
 
 
 def solution(mesh):

time: 87.2 us -> 83 us (0.952)
  Pallas kernels: 87.1 us -> 82.9 us
    pallas_call x1, Pallas kernels: 84.1 us -> 81.1 us  [body(): pl.pallas_call(mixer, out_shape=(jax.ShapeDtypeStruct((2 * D, B), F32), j...]
    pallas_call x1, Pallas kernels: 3.06 us -> 1.74 us  [body(): pl.pallas_call(projector, out_shape=jax.ShapeDtypeStruct((D, 2, B), BF16)...]
where the time goes in v1:
time: 83 us; the launch traced here: 82.9 us
  Pallas kernels  82.9 us (100%)
    pallas_call x1, Pallas kernels, body(): pl.pallas_call(mixer, out_shape=(jax.ShapeDtypeStruct((2 * D, B), F32), j...  81.1 us
    pallas_call x1, Pallas kernels, body(): pl.pallas_call(projector, out_shape=jax.ShapeDtypeStruct((D, 2, B), BF16)...  1.74 us

profile of v1, /device:TPU:1, one launch (start us, length us, event | category | flops | bytes accessed | tf_op | source)
XLA Modules:
  0.0 82.9 jit_solution(1706321323876664823)
XLA Ops:
  0.0 81.1 %shard_map.100 = (f32[768,1024]{1,0:T(8,128)S(1)}, bf16[768,128]{1,0:T(8,128)(2,1)S(1)}, bf16[128,1024]{1,0:T(8,128)(2,1)S(1)}) custom-call(bf16[48,16,1024]{2,1,0:T(8,128)(2,1)} %tok_h.1, bf16[384,2,1024]{2,1,0:T(2,128)(2,1)} %gat_h.1, bf16[48,32,512]{2,1,0:T(8,128)(2,1)} %ker_h.1, bf16[1024,1024]{1,0:T(8,128)(2,1)} %f1_h.1, f32[16,1024]{1,0:T(8,128)} %tw1_h.1, ...), custom_call_target="tpu_custom_call" | custom-call | tf_op jit(solution)/shard_map/pallas_call | solution.py:312
  81.2 1.7 %shard_map.101 = bf16[384,2,1024]{2,1,0:T(2,128)(2,1)} custom-call(f32[768,1024]{1,0:T(8,128)S(1)} %get-tuple-element.8.acc, bf16[768,128]{1,0:T(8,128)(2,1)S(1)} %get-tuple-element.9.pb5, bf16[128,1024]{1,0:T(8,128)(2,1)S(1)} %get-tuple-element.10.g5), custom_call_target="tpu_custom_call" | custom-call | tf_op jit(solution)/shard_map/pallas_call | solution.py:336

commit v2 on v1

--- a/solution.py
+++ b/solution.py
@@ -19,6 +19,8 @@
 NQ = CL // CQ
 W = CQ * KL
 FAR = [d for k in range(17) for d in sorted({16 - k, 16 + k}) if 0 < d < SEQ]
+
+EARLY = [z * 4 + y * 2 + c for y in (0, 1) for z in range(4) for c in (0, 1)] + list(range(16, SEQ))
 
 
 def nt(a, b):
@@ -172,20 +174,11 @@
                 device_id={"chan": p}, device_id_type=MESH,
             ).start()
 
-    r4 = lax.rem(me, 4)
-
-    def group(q, zs):
-        for zz in zs:
-            for dr in range(4):
-                p = zz * 4 + lax.rem(r4 + dr, 4)
-
-                @pl.when(p != me)
-                def _(p=p):
-                    send(snd2, zin, zsem.at[q], p, at(q, W))
-
-    def far(q):
-        for d in FAR:
-            send(snd2, zin, zsem.at[q], lax.rem(me + d, SEQ), at(q, W))
+    def group(q):
+        for p in EARLY:
+            @pl.when(p != me)
+            def _(p=p):
+                send(snd2, zin, zsem.at[q], p, at(q, W))
 
     def onward(q):
         block = cin.at[q, pl.ds(0, CHAN - 1)]
@@ -203,7 +196,7 @@
             lax.fori_loop(0, SEQ, pick, 0, unroll=8)
         lanes = at(q, W)
         zin[me, :, lanes] = snd2[me, :, lanes]
-        group(q, range(8))
+        group(q)
 
     def gate_rows(i, c):
         g = gat[i].astype(F32)

time: 83 us -> 82 us (0.988)
  Pallas kernels: 82.9 us -> 81.9 us
    pallas_call x1, Pallas kernels: 81.1 us -> 80.1 us  [body(): pl.pallas_call(mixer, out_shape=(jax.ShapeDtypeStruct((2 * D, B), F32), j...]
where the time goes in v2:
time: 82 us; the launch traced here: 81.9 us
  Pallas kernels  81.9 us (100%)
    pallas_call x1, Pallas kernels, body(): pl.pallas_call(mixer, out_shape=(jax.ShapeDtypeStruct((2 * D, B), F32), j...  80.1 us
    pallas_call x1, Pallas kernels, body(): pl.pallas_call(projector, out_shape=jax.ShapeDtypeStruct((D, 2, B), BF16)...  1.74 us

profile of v2, /device:TPU:1, one launch (start us, length us, event | category | flops | bytes accessed | tf_op | source)
XLA Modules:
  0.0 81.9 jit_solution(18309300185235198341)
XLA Ops:
  0.0 80.1 %shard_map.100 = (f32[768,1024]{1,0:T(8,128)S(1)}, bf16[768,128]{1,0:T(8,128)(2,1)S(1)}, bf16[128,1024]{1,0:T(8,128)(2,1)S(1)}) custom-call(bf16[48,16,1024]{2,1,0:T(8,128)(2,1)} %tok_h.1, bf16[384,2,1024]{2,1,0:T(2,128)(2,1)} %gat_h.1, bf16[48,32,512]{2,1,0:T(8,128)(2,1)} %ker_h.1, bf16[1024,1024]{1,0:T(8,128)(2,1)} %f1_h.1, f32[16,1024]{1,0:T(8,128)} %tw1_h.1, ...), custom_call_target="tpu_custom_call" | custom-call | tf_op jit(solution)/shard_map/pallas_call | solution.py:305
  80.1 1.7 %shard_map.101 = bf16[384,2,1024]{2,1,0:T(2,128)(2,1)} custom-call(f32[768,1024]{1,0:T(8,128)S(1)} %get-tuple-element.8.acc, bf16[768,128]{1,0:T(8,128)(2,1)S(1)} %get-tuple-element.9.pb5, bf16[128,1024]{1,0:T(8,128)(2,1)S(1)} %get-tuple-element.10.g5), custom_call_target="tpu_custom_call" | custom-call | tf_op jit(solution)/shard_map/pallas_call | solution.py:329

commit v3 on v2

--- a/solution.py
+++ b/solution.py
@@ -287,11 +287,11 @@
 
 def projector(acc, pb5, g5, out_h, res, sem):
     copies = []
-    for n in range(B // 256):
-        cols = slice(n * 256, (n + 1) * 256)
+    for n in range(B // PIECE):
+        cols = slice(n * PIECE, (n + 1) * PIECE)
         v = acc[:, cols] + jnp.dot(pb5[...], g5[:, cols], preferred_element_type=F32)
-        res[n] = v.astype(BF16).reshape(D, 2, 256)
-        copies.append(pltpu.make_async_copy(res.at[n], out_h.at[:, :, pl.ds(n * 256, 256)], sem.at[n]))
+        res[n] = v.astype(BF16).reshape(D, 2, PIECE)
+        copies.append(pltpu.make_async_copy(res.at[n], out_h.at[:, :, pl.ds(n * PIECE, PIECE)], sem.at[n]))
         copies[-1].start()
     for c in copies:
         c.wait()
@@ -331,13 +331,14 @@
         out_shape=jax.ShapeDtypeStruct((D, 2, B), BF16),
         in_specs=[whole, whole, whole],
         out_specs=hbm,
-        scratch_shapes=[vm((B // 256, D, 2, 256), BF16), dma((B // 256,))],
+        scratch_shapes=[vm((B // PIECE, D, 2, PIECE), BF16), dma((B // PIECE,))],
         compiler_params=pltpu.CompilerParams(vmem_limit_bytes=32 * 1024 * 1024),
     )(*parts)
 
 
 VLIM = 48
 UNROLL = True
+PIECE = 512
 
 
 def solution(mesh):

time: 82 us -> 81.7 us (level)
  no operation moved by 1% of the time
where the time goes in v3:
time: 81.7 us
  Pallas kernels  81.6 us (100%)
    pallas_call x1, Pallas kernels, body(): pl.pallas_call(mixer, out_shape=(jax.ShapeDtypeStruct((2 * D, B), F32), j...  80.1 us

profile of v3, /device:TPU:1, one launch (start us, length us, event | category | flops | bytes accessed | tf_op | source)
XLA Modules:
  0.0 81.7 jit_solution(15929915711324347988)
XLA Ops:
  0.0 80.1 %shard_map.100 = (f32[768,1024]{1,0:T(8,128)S(1)}, bf16[768,128]{1,0:T(8,128)(2,1)S(1)}, bf16[128,1024]{1,0:T(8,128)(2,1)S(1)}) custom-call(bf16[48,16,1024]{2,1,0:T(8,128)(2,1)} %tok_h.1, bf16[384,2,1024]{2,1,0:T(2,128)(2,1)} %gat_h.1, bf16[48,32,512]{2,1,0:T(8,128)(2,1)} %ker_h.1, bf16[1024,1024]{1,0:T(8,128)(2,1)} %f1_h.1, f32[16,1024]{1,0:T(8,128)} %tw1_h.1, ...), custom_call_target="tpu_custom_call" | custom-call | tf_op jit(solution)/shard_map/pallas_call | solution.py:305
  80.1 1.5 %shard_map.101 = bf16[384,2,1024]{2,1,0:T(2,128)(2,1)} custom-call(f32[768,1024]{1,0:T(8,128)S(1)} %get-tuple-element.8.acc, bf16[768,128]{1,0:T(8,128)(2,1)S(1)} %get-tuple-element.9.pb5, bf16[128,1024]{1,0:T(8,128)(2,1)S(1)} %get-tuple-element.10.g5), custom_call_target="tpu_custom_call" | custom-call | tf_op jit(solution)/shard_map/pallas_call | solution.py:329
